TPU v7x, 256 devices: a whole 4x4x8 slice. The times are simulated.
256 devices in a mesh: seq: 128 (over x_lo, z, y, core), mp: 2 (over x_hi).
Axes of the slice: x: 4 (x_hi: 2, x_lo: 2; x = x_hi * 2 + x_lo), y: 4, z: 8, core: 2. Of those that a mesh axis runs over, the one named last changes fastest.
Arguments:
- patches: bfloat16 [32768, 64], P('seq'), may hold values from -6 to 6
- clip_shape: int32 [64, 3], replicated, may hold values from 1 to 16, as said below
- shard_counts: int32 [128], replicated, may hold values from 1 to 256, as said below
- patch_weight: bfloat16 [64, 2560], P(None, 'mp'), may hold values from -3 to 3
- patch_bias: float32 [2560], P('mp'), may hold values from -6 to 6
- time_mod: float32 [64, 2, 2560], P(None, None, 'mp'), may hold values from -6 to 6
- block_mod: float32 [2, 2560], P(None, 'mp'), may hold values from -4 to 4
- w_query: bfloat16 [2560, 2560], P('seq', 'mp'), may hold values from -0.47434165 to 0.47434165
- query_bias: float32 [2560], P('mp'), may hold values from -4 to 4
- w_keyvalue: bfloat16 [2560, 5120], P('seq', 'mp'), may hold values from -0.47434165 to 0.47434165
- keyvalue_bias: float32 [5120], P('mp'), may hold values from -6 to 6
- norm_gain: float32 [2, 2560], P(None, 'mp'), may hold values from 1 to 2
Outputs:
- attention: bfloat16 [32768, 2560], P('seq', 'mp')
Inputs may be any that keep to these rules, and one draw needn't show every extreme that they name: `clip_shape`: clip c lies on shards 2 c to 2 c + 1. Frames run from 1 to 2, patch rows from 8 to 16, patch columns from 8 to 16; some clip has 2 frames of 16 by 16 patches. `shard_counts`: the counts of clip c's 2 shards add up to the product of clip_shape[c].
All inputs are finite; a program needn't handle non-finite values.
Results may differ from a plain program's by a relative error of at most 0.0063.
Values may be sent and summed in bfloat16 or wider, within the bound.
A program may use at most 128 MiB of HBM per device.

v0:
```python
import math
import jax
import jax.numpy as jnp
from jax import lax
from jax.sharding import PartitionSpec as P

D = 2560
HEADS = 20
HD = 128
GROUP = 2
EPSILON = 1e-06


def partner_2(value, axis, apart):
    mask = 2**apart
    pairs = [(source, source ^ mask) for source in range(lax.axis_size(axis))]
    return lax.ppermute(value, axis, pairs)


def token_places(group_counts, member_ids, slot_ids, shape_row):
    before = jnp.cumsum(group_counts) - group_counts
    lookup = jnp.arange(GROUP, dtype=jnp.int32)[None, :] == member_ids[:, None]
    offset = jnp.sum(jnp.where(lookup, before[None, :], 0), axis=1)
    holding = jnp.sum(jnp.where(lookup, group_counts[None, :], 0), axis=1)
    position = offset + slot_ids
    plane_size = shape_row[1] * shape_row[2]
    frame_pos = position // plane_size
    row_pos = position // shape_row[2] % shape_row[1]
    col_pos = position % shape_row[2]
    return (slot_ids < holding, frame_pos, row_pos, col_pos)


def rotary_tables(frame_pos, row_pos, col_pos):
    other_pairs = HD // 6
    frame_pairs = HD // 2 - 2 * other_pairs
    pair_id = jnp.arange(HD, dtype=jnp.int32) // 2
    in_frame = pair_id < frame_pairs
    in_row = jnp.logical_and(pair_id >= frame_pairs, pair_id < frame_pairs + other_pairs)
    within = jnp.where(
        in_frame,
        pair_id,
        jnp.where(in_row, pair_id - frame_pairs, pair_id - frame_pairs - other_pairs),
    ).astype(jnp.float32)
    axis_span = jnp.where(in_frame, 2.0 * frame_pairs, 2.0 * other_pairs).astype(jnp.float32)
    inverse = jnp.exp(-(2.0 * within / axis_span) * math.log(10000.0))
    position = jnp.where(
        in_frame[None, :],
        frame_pos[:, None],
        jnp.where(in_row[None, :], row_pos[:, None], col_pos[:, None]),
    ).astype(jnp.float32)
    angles = position * inverse[None, :]
    return (jnp.cos(angles), jnp.sin(angles))


def rotate_pairs(values, cosine_table, sine_table):
    parity = jnp.arange(HD, dtype=jnp.int32) % 2 == 0
    partner = jnp.where(parity, -jnp.roll(values, -1, axis=-1), jnp.roll(values, 1, axis=-1))
    return values * cosine_table[:, None, :] + partner * sine_table[:, None, :]


def modulate_rows(embedded, row_sums, squares, modulation):
    average = row_sums / D
    variance = squares / D - average * average
    normed = (embedded - average[:, None]) * lax.rsqrt(variance[:, None] + EPSILON)
    return (normed * (1.0 + modulation[1]) + modulation[0]).astype(jnp.bfloat16)


def finish_heads(raw_rows, squares, scale_gain, cosine_table, sine_table):
    normed = raw_rows * lax.rsqrt(squares[:, None] / (HEADS * HD) + EPSILON) * scale_gain
    return rotate_pairs(normed.reshape(raw_rows.shape[0], -1, HD), cosine_table, sine_table).astype(
        jnp.bfloat16
    )


def contract(left_rows, pieces):
    return jnp.dot(left_rows, pieces, preferred_element_type=jnp.float32)


def split_pairs(pair_acc, keyvalue_bias, heads_here):
    tokens = pair_acc.shape[0]
    pair_raw = (pair_acc + keyvalue_bias).reshape(tokens, heads_here, 2, HD)
    key_raw = pair_raw[:, :, 0].reshape(tokens, heads_here * HD)
    value_rows = pair_raw[:, :, 1].reshape(tokens, heads_here * HD).astype(jnp.bfloat16)
    return (key_raw, value_rows)


def count_of(group_counts, source):
    return jnp.sum(jnp.where(jnp.arange(GROUP, dtype=jnp.int32) == source, group_counts, 0))


def gather_group(key_rows, value_rows, member):
    tokens = value_rows.shape[0]
    blocks = jnp.stack([key_rows.reshape(tokens, -1), value_rows])
    sources = [member]
    partner = partner_2(blocks, "seq", 0)
    blocks = jnp.concatenate([blocks, partner], axis=1)
    sources = sources + [jnp.bitwise_xor(source, 1 << 0) for source in sources]
    return (blocks, sources)


def attend_rows(queries, all_keys, all_values, key_valid):
    scores = jnp.einsum(
        "qhd,khd->hqk", queries, all_keys, preferred_element_type=jnp.float32
    ) * HD ** (-0.5)
    weights = jnp.where(key_valid[None, None, :], jnp.exp(scores), 0.0)
    totals = jnp.sum(weights, axis=-1)
    numerator = jnp.einsum(
        "hqk,khd->qhd", weights.astype(jnp.bfloat16), all_values, preferred_element_type=jnp.float32
    )
    return numerator / jnp.transpose(totals)[:, :, None]


def shards(
    patches,
    clip_shape,
    shard_counts,
    patch_weight,
    patch_bias,
    time_mod,
    block_mod,
    w_query,
    query_bias,
    w_keyvalue,
    keyvalue_bias,
    norm_gain,
):
    tokens = patches.shape[0]
    heads_here = w_query.shape[1] // HD
    seq_index = lax.axis_index("seq")
    clip_id = seq_index // GROUP
    member = seq_index % GROUP
    group_counts = lax.dynamic_slice_in_dim(shard_counts, clip_id * GROUP, GROUP, 0)
    shape_row = lax.dynamic_index_in_dim(clip_shape, clip_id, 0, keepdims=False)
    slot_ids = jnp.arange(tokens, dtype=jnp.int32)
    is_valid, frame_pos, row_pos, col_pos = token_places(
        group_counts, jnp.full((tokens,), member, jnp.int32), slot_ids, shape_row
    )
    modulation = lax.dynamic_index_in_dim(time_mod, clip_id, 0, keepdims=False) + block_mod
    embedded = jnp.dot(patches, patch_weight, preferred_element_type=jnp.float32) + patch_bias
    row_sums, squares = lax.psum(
        (jnp.sum(embedded, axis=1), jnp.sum(embedded * embedded, axis=1)), "mp"
    )
    half_rows = modulate_rows(embedded, row_sums, squares, modulation)
    hidden = lax.all_gather(half_rows, "mp", axis=1, tiled=True)
    cosine_table, sine_table = rotary_tables(frame_pos, row_pos, col_pos)
    query_acc = contract(hidden, lax.all_gather(w_query, "seq", axis=0, tiled=True))
    pair_acc = contract(hidden, lax.all_gather(w_keyvalue, "seq", axis=0, tiled=True))
    query_raw = query_acc + query_bias
    key_raw, value_rows = split_pairs(pair_acc, keyvalue_bias, heads_here)
    query_squares, key_squares = lax.psum(
        (jnp.sum(query_raw * query_raw, axis=1), jnp.sum(key_raw * key_raw, axis=1)), "mp"
    )
    queries = finish_heads(query_raw, query_squares, norm_gain[0], cosine_table, sine_table)
    key_rows = finish_heads(key_raw, key_squares, norm_gain[1], cosine_table, sine_table)
    blocks, sources = gather_group(key_rows, value_rows, member)
    key_valid = jnp.concatenate([slot_ids < count_of(group_counts, source) for source in sources])
    all_keys = blocks[0].reshape(-1, heads_here, HD)
    all_values = blocks[1].reshape(-1, heads_here, HD)
    result = attend_rows(queries, all_keys, all_values, key_valid)
    result = jnp.where(is_valid[:, None, None], result, 0.0)
    return result.reshape(tokens, heads_here * HD).astype(jnp.bfloat16)


def solution(mesh):
    return jax.shard_map(
        shards,
        mesh=mesh,
        in_specs=(
            P("seq", None),
            P(),
            P(),
            P(None, "mp"),
            P("mp"),
            P(None, None, "mp"),
            P(None, "mp"),
            P("seq", "mp"),
            P("mp"),
            P("seq", "mp"),
            P("mp"),
            P(None, "mp"),
        ),
        out_specs=P("seq", "mp"),
        check_vma=False,
    )
```

profile of v0, /device:TPU:1, one launch (start us, length us, event | category | flops | bytes accessed | tf_op | source)
XLA Modules:
  0.0 569.0 jit_solution(236258735546962702)
XLA Ops:
  6.5 0.0 copy-start
  6.5 0.0 all-gather.10.cloned.1.call-start
  6.5 0.7 all-gather.10.cloned.1.call-update
  7.3 0.0 all-gather.6.cloned.1.call-start
  7.3 0.1 copy-done
  7.5 1.2 fusion.33
  8.7 5.9 %all-reduce.1 = (f32[256]{0:T(256)S(1)}, f32[256]{0:T(256)S(1)}) all-reduce(f32[256]{0:T(256)S(1)} %get-tuple-element.6, f32[256]{0:T(256)S(1)} %get-tuple-element.5), channel_id=1, replica_groups=mesh['seq'=128,'mp'=2] {'mp'}, use_global_device_ids=true, to_apply=%region_4.5 | all-reduce | flops 512 | bytes 4096 | tf_op jit(solution)/shard_map/psum | solution.py:140
  14.6 0.0 copy-done.7
  14.6 0.7 bitcast_add_fusion
  15.3 0.0 copy-start.9
  15.3 0.0 copy-start.10
  15.4 0.0 copy-start.8
  15.4 1.1 add_convert_fusion
  16.5 0.0 all-gather.6.cloned.1.call-update
  16.5 0.0 all-gather.8.cloned.1.call-start
  16.6 0.7 all-gather.8.cloned.1.call-update
  17.3 0.0 copy-done.9
  17.3 0.1 constant_dynamic-slice_fusion
  17.4 0.6 fusion.39
  21.0 0.0 copy-done.10
  21.1 0.8 select_reduce_fusion.2
  21.8 0.2 reduce-window.9
  23.3 1.3 iota_compare_fusion
  24.7 0.1 select_reduce_fusion.1
  24.8 0.8 and_select_fusion.4
  25.6 0.6 fusion.26
  26.1 0.0 copy-start.12
  26.2 205.1 %all-gather.10.cloned.1.call-done = bf16[128,20,1280]{2,1,0:T(8,128)(2,1)} async-done(((bf16[1,20,1280]{2,1,0:T(8,128)(2,1)}), bf16[128,20,1280]{2,1,0:T(8,128)(2,1)}) %all-gather.10.cloned.1.call-update) | async-done | bytes 6553616 | tf_op jit(solution)/shard_map/all_gather | solution.py:146
  231.3 10.6 %reshape.424 = bf16[2560,1280]{1,0:T(8,128)(2,1)} reshape(bf16[128,20,1280]{2,1,0:T(8,128)(2,1)} %all-gather.10.cloned.1.call-done) | data formatting | bytes 13107200
  241.9 20.6 %all-gather.6.cloned.1.call-done = bf16[256,2560]{1,0:T(8,128)(2,1)} async-done(((bf16[256,1280]{1,0:T(8,128)(2,1)}), bf16[256,2560]{1,0:T(8,128)(2,1)}) %all-gather.6.cloned.1.call-update) | async-done | bytes 1310736 | tf_op jit(solution)/shard_map/all_gather | solution.py:144
  262.6 6.2 %multiply_reduce_fusion = (f32[256]{0:T(256)S(1)}, f32[256,1280]{1,0:T(8,128)}) fusion(f32[1280]{0:T(1024)S(1)} %copy-done.12, bf16[256,2560]{1,0:T(8,128)(2,1)} %all-gather.6.cloned.1.call-done, bf16[2560,1280]{1,0:T(8,128)(2,1)} %reshape.424), kind=kOutput, calls=%fused_computation.31 | convolution fusion | flops 1678704384 | bytes 9181184 | tf_op jit(solution)/shard_map/dot_general | solution.py:76
  268.7 222.9 %all-gather.8.cloned.1.call-done = bf16[128,20,2560]{2,1,0:T(8,128)(2,1)} async-done(((bf16[1,20,2560]{2,1,0:T(8,128)(2,1)}), bf16[128,20,2560]{2,1,0:T(8,128)(2,1)}) %all-gather.8.cloned.1.call-update) | async-done | bytes 13107216 | tf_op jit(solution)/shard_map/all_gather | solution.py:147
  491.7 18.0 %reshape.422 = bf16[2560,2560]{1,0:T(8,128)(2,1)} reshape(bf16[128,20,2560]{2,1,0:T(8,128)(2,1)} %all-gather.8.cloned.1.call-done) | data formatting | bytes 26214400
  509.7 0.0 copy-done.11
  509.7 7.0 %convolution_add_fusion = f32[256,2560]{1,0:T(8,128)S(1)} fusion(bf16[256,2560]{1,0:T(8,128)(2,1)} %all-gather.6.cloned.1.call-done, bf16[2560,2560]{1,0:T(8,128)(2,1)} %reshape.422, f32[2560]{0:T(1024)S(1)} %copy-done.11), kind=kOutput, calls=%fused_computation.3 | convolution fusion | flops 3356098560 | bytes 17049600 | tf_op jit(solution)/shard_map/dot_general | solution.py:76
  516.7 2.8 reshape.417
  519.5 2.6 slice.84
  522.1 0.2 multiply_reduce_fusion.1
  522.3 5.5 all-reduce
  527.8 0.2 fusion.16
  528.0 1.5 fusion.37
  529.5 2.0 fusion.38
  531.5 2.1 copy.42
  533.6 4.3 slice.89
  538.0 1.5 maximum_negate_fusion
  539.5 2.9 copy.43
  542.3 1.5 pad_maximum_fusion.1
  543.9 2.9 copy.44
  546.8 0.0 copy-done.3
  546.8 1.0 copy.54
  547.7 2.5 fusion.15
  550.3 0.0 copy-start.6
  550.3 1.2 pad_maximum_fusion.2
  551.5 2.3 collective-permute-start
  553.7 1.3 multiply_multiply_fusion
  555.0 1.7 copy.46
  556.7 0.3 fusion.36
  557.0 0.0 collective-permute-done
  557.0 1.5 pad_maximum_fusion
  558.5 0.2 fusion.34
  558.7 1.6 fusion
  560.3 0.0 copy-start.1
  560.4 1.0 select_convert_fusion
  561.4 1.1 copy.49
  (26 shorter events, 0.2 us)
Async XLA Ops:
  6.5 0.9 copy-start
  6.5 8.0 %copy-start.7 = (f32[2,1280]{1,0:T(2,128)S(1)}, f32[2,1280]{1,0:T(2,128)}, u32[]{:S(2)}) copy-start(f32[2,1280]{1,0:T(2,128)} %param.18) | copy-start | bytes 30724
  6.5 224.8 %all-gather.10.cloned.1.call-start = ((), (), s32[]{:S(2)}) async-start(), calls=%async_computation.2 | async-start | bytes 7925760 | tf_op jit(solution)/shard_map/all_gather | solution.py:146
  7.3 255.3 %all-gather.6.cloned.1.call-start = ((), (), s32[]{:S(2)}) async-start(), calls=%async_computation | async-start | bytes 1966080 | tf_op jit(solution)/shard_map/all_gather | solution.py:144
  15.3 1.9 copy-start.9
  15.3 5.7 %copy-start.10 = (s32[128]{0:T(128)S(1)}, s32[128]{0:T(128)}, u32[]{:S(2)}) copy-start(s32[128]{0:T(128)} %param.14) | copy-start | bytes 1540
  15.4 9.2 %copy-start.8 = (f32[2,1280]{1,0:T(2,128)S(1)}, f32[2,1280]{1,0:T(2,128)}, u32[]{:S(2)}) copy-start(f32[2,1280]{1,0:T(2,128)} %param.23) | copy-start | bytes 30724
  16.5 475.1 %all-gather.8.cloned.1.call-start = ((), (), s32[]{:S(2)}) async-start(), calls=%async_computation.1 | async-start | bytes 15851520 | tf_op jit(solution)/shard_map/all_gather | solution.py:147
  26.1 236.4 %copy-start.12 = (f32[1280]{0:T(1024)S(1)}, f32[1280]{0:T(1024)}, u32[]{:S(2)}) copy-start(f32[1280]{0:T(1024)} %param.20) | copy-start | bytes 15364
  268.7 241.0 %copy-start.11 = (f32[2560]{0:T(1024)S(1)}, f32[2560]{0:T(1024)}, u32[]{:S(2)}) copy-start(f32[2560]{0:T(1024)} %param.22) | copy-start | bytes 30724
  533.6 4.3 copy-start.4
  533.6 4.3 copy-start.5
  539.5 2.9 copy-start.2
  543.9 2.9 copy-start.3
  550.3 3.5 copy-start.6
  551.5 5.6 collective-permute-start
  560.3 2.1 copy-start.1
Sparse Core Ops, SparseCore 0:
  9.2 222.0 all-gather.9
  233.1 29.4 all-gather.5
  264.4 227.1 all-gather.7
where the time goes:
time: 570 us; the launch traced here: 569 us
  waiting for transfers between devices  450 us (79%)
  local copies, waits for them, and re-layouts  55 us (10%)
  between operations  17.7 us (3%)
  matrix products  17.1 us (3%)
  other arithmetic  15.4 us (3%)
  blocking collectives  11.3 us (2%)
    all_gather x1, waiting for transfers between devices, shards(): lax.all_gather(w_keyvalue, 'seq', axis=0, tiled=True)  223 us
    all_gather x1, waiting for transfers between devices, shards(): lax.all_gather(w_query, 'seq', axis=0, tiled=True)  205 us
    unnamed x29, local copies, waits for them, and re-layouts  29.8 us
    all_gather x1, waiting for transfers between devices, shards(): hidden = lax.all_gather(half_rows, 'mp', axis=1, tiled=True)  20.6 us
    dot_general x2, matrix products, contract(): return jnp.dot(left_rows, pieces, preferred_element_type=jnp.float32)  13.2 us
  transfers between devices with their start and end apart: 4, of which 3 were waited for; matrix products, arithmetic and copies ran while one was open for 5% of the time, Pallas kernels for 0%

commit v1 on v0

--- a/solution.py
+++ b/solution.py
@@ -9,6 +9,11 @@
 HD = 128
 GROUP = 2
 EPSILON = 1e-06
+
+
+def gather_over(x, axis, d):
+    outgoing = jnp.stack([x] * lax.axis_size(axis))
+    return jnp.concatenate(lax.all_to_all(outgoing, axis, 0, 0), axis=d)
 
 
 def partner_2(value, axis, apart):
@@ -143,7 +148,7 @@
     half_rows = modulate_rows(embedded, row_sums, squares, modulation)
     hidden = lax.all_gather(half_rows, "mp", axis=1, tiled=True)
     cosine_table, sine_table = rotary_tables(frame_pos, row_pos, col_pos)
-    query_acc = contract(hidden, lax.all_gather(w_query, "seq", axis=0, tiled=True))
+    query_acc = contract(hidden, gather_over(w_query, "seq", 0))
     pair_acc = contract(hidden, lax.all_gather(w_keyvalue, "seq", axis=0, tiled=True))
     query_raw = query_acc + query_bias
     key_raw, value_rows = split_pairs(pair_acc, keyvalue_bias, heads_here)

time: 570 us -> 456 us (0.80)
  waiting for transfers between devices: 450 us -> 312 us
  starting transfers between devices: 2.35 us -> 18.3 us
    all_gather x1 -> x0, waiting for transfers between devices: 205 us -> none  [shards(): lax.all_gather(w_query, 'seq', axis=0, tiled=True)]
    all_to_all x0 -> x1, waiting for transfers between devices: none -> 194 us  [gather_over(): return jnp.concatenate(lax.all_to_all(outgoing, axis, 0, 0), axis=d)]
    all_gather x1, waiting for transfers between devices: 223 us -> 118 us  [shards(): lax.all_gather(w_keyvalue, 'seq', axis=0, tiled=True)]
    all_gather x1, waiting for transfers between devices: 20.6 us -> 0.01 us  [shards(): hidden = lax.all_gather(half_rows, 'mp', axis=1, tiled=True)]
    all_to_all x0 -> x1, starting transfers between devices: none -> 16 us  [gather_over(): return jnp.concatenate(lax.all_to_all(outgoing, axis, 0, 0), axis=d)]
    reshape x0 -> x1, local copies, waits for them, and re-layouts: none -> 10.6 us  [gather_over(): return jnp.concatenate(lax.all_to_all(outgoing, axis, 0, 0), axis=d)]
    unnamed x29 -> x28, local copies, waits for them, and re-layouts: 29.8 us -> 19.2 us
  transfers between devices with their start and end apart: 4 -> 4, of which waited for: 3 -> 2; matrix products, arithmetic and copies ran while one was open for 5% -> 6% of each run, Pallas kernels for 0% -> 0%
where the time goes in v1:
time: 456 us; the launch traced here: 453 us
  waiting for transfers between devices  312 us (68%)
  local copies, waits for them, and re-layouts  57.4 us (13%)
  starting transfers between devices  18.3 us (4%)
  other arithmetic  18.3 us (4%)
  between operations  17.8 us (4%)
  matrix products  17.1 us (4%)
  blocking collectives  11.3 us (2%)
    all_to_all x1, waiting for transfers between devices, gather_over(): return jnp.concatenate(lax.all_to_all(outgoing, axis, 0, 0), axis=d)  194 us
    all_gather x1, waiting for transfers between devices, shards(): lax.all_gather(w_keyvalue, 'seq', axis=0, tiled=True)  118 us
    unnamed x28, local copies, waits for them, and re-layouts  19.2 us
    all_to_all x1, starting transfers between devices, gather_over(): return jnp.concatenate(lax.all_to_all(outgoing, axis, 0, 0), axis=d)  16 us
    dot_general x2, matrix products, contract(): return jnp.dot(left_rows, pieces, preferred_element_type=jnp.float32)  13.2 us
    reshape x1, local copies, waits for them, and re-layouts, gather_over(): return jnp.concatenate(lax.all_to_all(outgoing, axis, 0, 0), axis=d)  10.6 us
  transfers between devices with their start and end apart: 4, of which 2 were waited for; matrix products, arithmetic and copies ran while one was open for 6% of the time, Pallas kernels for 0%

profile of v1, /device:TPU:1, one launch (start us, length us, event | category | flops | bytes accessed | tf_op | source)
XLA Modules:
  0.0 452.6 jit_solution(13002182191155310422)
XLA Ops:
  6.5 0.0 copy-start
  6.5 0.0 all-gather.4.cloned.1.call-start
  6.5 0.8 bitcast_add_fusion
  7.3 0.1 copy-done
  7.5 1.2 fusion.33
  8.7 5.9 %all-reduce.1 = (f32[256]{0:T(256)S(1)}, f32[256]{0:T(256)S(1)}) all-reduce(f32[256]{0:T(256)S(1)} %get-tuple-element.6, f32[256]{0:T(256)S(1)} %get-tuple-element.5), channel_id=1, replica_groups=mesh['seq'=128,'mp'=2] {'mp'}, use_global_device_ids=true, to_apply=%region_4.5 | all-reduce | flops 512 | bytes 4096 | tf_op jit(solution)/shard_map/psum | solution.py:145
  14.6 1.1 add_convert_fusion
  15.7 0.0 all-gather.4.cloned.1.call-update
  15.8 0.0 all-gather.6.cloned.1.call-start
  15.8 0.7 all-gather.6.cloned.1.call-update
  16.5 0.0 copy-done.7
  16.5 3.7 stack.5
  20.2 16.0 %all-to-all-start = ((bf16[128,20,1280]{2,1,0:T(8,128)(2,1)}), bf16[128,20,1280]{2,1,0:T(8,128)(2,1)}, u32[]{:S(2)}, u32[]{:S(2)}) async-start(bf16[128,20,1280]{2,1,0:T(8,128)(2,1)} %stack.5), calls=%async_computation | async-start | bytes 15728640 | tf_op jit(solution)/shard_map/all_to_all | solution.py:16
  36.2 0.0 copy-done.9
  36.2 0.1 constant_dynamic-slice_fusion
  36.3 0.5 fusion.39
  39.8 0.0 copy-done.10
  39.8 0.8 select_reduce_fusion.2
  40.6 0.2 reduce-window.9
  42.0 1.4 iota_compare_fusion
  43.4 0.0 copy-done.8
  43.4 0.1 select_reduce_fusion.1
  43.5 0.8 and_select_fusion.4
  44.3 0.6 fusion.26
  44.9 0.0 copy-start.12
  44.9 193.6 %all-to-all-done = bf16[128,20,1280]{2,1,0:T(8,128)(2,1)} async-done(((bf16[128,20,1280]{2,1,0:T(8,128)(2,1)}), bf16[128,20,1280]{2,1,0:T(8,128)(2,1)}, u32[]{:S(2)}, u32[]{:S(2)}) %all-to-all-start) | async-done | bytes 6553632 | tf_op jit(solution)/shard_map/all_to_all | solution.py:16
  238.6 10.6 %reshape.425 = bf16[2560,1280]{1,0:T(8,128)(2,1)} reshape(bf16[128,20,1280]{2,1,0:T(8,128)(2,1)} %all-to-all-done) | data formatting | bytes 13107200 | tf_op jit(solution)/shard_map/reshape | solution.py:16
  249.2 0.0 copy-done.12
  249.2 6.2 %multiply_reduce_fusion = (f32[256]{0:T(256)S(1)}, f32[256,1280]{1,0:T(8,128)}) fusion(f32[1280]{0:T(1024)S(1)} %copy-done.12, bf16[256,2560]{1,0:T(8,128)(2,1)} %all-gather.4.cloned.1.call-done, bf16[2560,1280]{1,0:T(8,128)(2,1)} %reshape.425), kind=kOutput, calls=%fused_computation.31 | convolution fusion | flops 1678704384 | bytes 9181184 | tf_op jit(solution)/shard_map/dot_general | solution.py:81
  255.5 118.0 %all-gather.6.cloned.1.call-done = bf16[128,20,2560]{2,1,0:T(8,128)(2,1)} async-done(((bf16[1,20,2560]{2,1,0:T(8,128)(2,1)}), bf16[128,20,2560]{2,1,0:T(8,128)(2,1)}) %all-gather.6.cloned.1.call-update) | async-done | bytes 13107216 | tf_op jit(solution)/shard_map/all_gather | solution.py:152
  373.5 18.0 %reshape.428 = bf16[2560,2560]{1,0:T(8,128)(2,1)} reshape(bf16[128,20,2560]{2,1,0:T(8,128)(2,1)} %all-gather.6.cloned.1.call-done) | data formatting | bytes 26214400
  391.5 0.0 copy-done.11
  391.5 7.0 %convolution_add_fusion = f32[256,2560]{1,0:T(8,128)S(1)} fusion(bf16[256,2560]{1,0:T(8,128)(2,1)} %all-gather.4.cloned.1.call-done, bf16[2560,2560]{1,0:T(8,128)(2,1)} %reshape.428, f32[2560]{0:T(1024)S(1)} %copy-done.11), kind=kOutput, calls=%fused_computation.3 | convolution fusion | flops 3356098560 | bytes 17049600 | tf_op jit(solution)/shard_map/dot_general | solution.py:81
  398.5 2.8 reshape.422
  401.3 2.8 slice.84
  404.1 0.0 copy-done.2
  404.1 2.4 slice.89
  406.6 0.2 multiply_reduce_fusion.1
  406.8 2.2 copy.42
  408.9 5.4 %all-reduce = (f32[256]{0:T(256)S(1)}, f32[256]{0:T(256)S(1)}) all-reduce(f32[256]{0:T(256)S(1)} %multiply_reduce_fusion.1, f32[256]{0:T(256)S(1)} %get-tuple-element.40), channel_id=1, replica_groups=mesh['seq'=128,'mp'=2] {'mp'}, use_global_device_ids=true, to_apply=%region_6.7 | all-reduce | flops 512 | bytes 4096 | tf_op jit(solution)/shard_map/psum | solution.py:155
  414.4 0.2 fusion.16
  414.6 2.0 fusion.38
  416.6 1.9 fusion.37
  418.5 0.0 copy-done.3
  418.5 1.0 copy.54
  419.5 3.3 maximum_negate_fusion
  422.8 2.9 copy.43
  425.7 0.0 copy-done.4
  425.7 2.8 pad_maximum_fusion.1
  428.5 2.9 copy.44
  431.4 2.1 fusion.15
  433.5 0.0 copy-start.6
  433.6 1.2 pad_maximum_fusion.2
  434.7 2.3 collective-permute-start
  437.0 1.3 multiply_multiply_fusion
  438.3 1.7 copy.46
  440.0 0.3 fusion.36
  440.3 0.0 collective-permute-done
  440.3 1.5 pad_maximum_fusion
  441.8 0.2 fusion.34
  442.0 1.6 fusion
  443.6 0.0 copy-start.1
  443.6 1.0 select_convert_fusion
  444.7 1.1 copy.49
  (26 shorter events, 0.2 us)
Async XLA Ops:
  6.5 0.9 copy-start
  6.5 242.7 %all-gather.4.cloned.1.call-start = ((), (), s32[]{:S(2)}) async-start(), calls=%async_computation.1 | async-start | bytes 1966080 | tf_op jit(solution)/shard_map/all_gather | solution.py:149
  14.6 1.9 copy-start.7
  15.8 357.7 %all-gather.6.cloned.1.call-start = ((), (), s32[]{:S(2)}) async-start(), calls=%async_computation.2 | async-start | bytes 15851520 | tf_op jit(solution)/shard_map/all_gather | solution.py:152
  20.2 16.0 %copy-start.9 = (s32[64,3]{0,1:T(4,128)S(1)}, s32[64,3]{0,1:T(4,128)}, u32[]{:S(2)}) copy-start(s32[64,3]{0,1:T(4,128)} %param.13) | copy-start | bytes 2308
  20.2 19.5 %copy-start.10 = (s32[128]{0:T(128)S(1)}, s32[128]{0:T(128)}, u32[]{:S(2)}) copy-start(s32[128]{0:T(128)} %param.14) | copy-start | bytes 1540
  20.2 23.2 %copy-start.8 = (f32[2,1280]{1,0:T(2,128)S(1)}, f32[2,1280]{1,0:T(2,128)}, u32[]{:S(2)}) copy-start(f32[2,1280]{1,0:T(2,128)} %param.23) | copy-start | bytes 30724
  20.2 218.3 %all-to-all-start = ((bf16[128,20,1280]{2,1,0:T(8,128)(2,1)}), bf16[128,20,1280]{2,1,0:T(8,128)(2,1)}, u32[]{:S(2)}, u32[]{:S(2)}) async-start(bf16[128,20,1280]{2,1,0:T(8,128)(2,1)} %stack.5), calls=%async_computation | async-start | bytes 15728640 | tf_op jit(solution)/shard_map/all_to_all | solution.py:16
  44.9 204.3 %copy-start.12 = (f32[1280]{0:T(1024)S(1)}, f32[1280]{0:T(1024)}, u32[]{:S(2)}) copy-start(f32[1280]{0:T(1024)} %param.20) | copy-start | bytes 15364
  255.5 136.1 %copy-start.11 = (f32[2560]{0:T(1024)S(1)}, f32[2560]{0:T(1024)}, u32[]{:S(2)}) copy-start(f32[2560]{0:T(1024)} %param.22) | copy-start | bytes 30724
  401.3 2.8 copy-start.2
  416.6 1.9 copy-start.3
  422.8 2.9 copy-start.4
  428.5 2.9 copy-start.5
  433.5 3.5 copy-start.6
  434.7 5.6 %collective-permute-start = (bf16[2,256,1280]{1,2,0:T(8,128)(2,1)}, bf16[2,256,1280]{1,2,0:T(8,128)(2,1)}, u32[]{:S(2)}, u32[]{:S(2)}) collective-permute-start(bf16[2,256,1280]{1,2,0:T(8,128)(2,1)} %pad_maximum_fusion.2), channel_id=1, source_target_pairs={{0,2},{2,0},{4,6},{6,4},{8,10},{10,8},{12,14},{14,12},{16,18},{18,... | collective-permute-start | bytes 3932168 | tf_op jit(solution)/shard_map/ppermute | solution.py:22
  443.6 2.1 copy-start.1
Sparse Core Ops, SparseCore 0:
  15.9 61.4 all-gather.3
  79.3 294.1 all-gather.5
